TPU v7x, 32 devices: a whole 2x2x4 slice. The times are simulated.
32 devices in a mesh: obs: 8 (over z, core), state: 4 (over y, x).
Axes of the slice: x: 2, y: 2, z: 4, core: 2. Of those that a mesh axis runs over, the one named last changes fastest.
Arguments:
- ensemble: bfloat16 [4, 1024, 256], P('state'), may hold values from -16 to 16
- obs_values: float32 [16384], P('obs'), may hold values from -72 to 72
- obs_error: float32 [16384], P('obs'), may hold values from 6 to 24
- h_blocks: bfloat16 [8, 4, 64, 128, 128], P('obs', 'state'), may hold values from -0.125 to 0.125
- block_rows: int32 [8, 4, 64], P('obs', 'state'), may hold values from 0 to 15
- block_cols: int32 [8, 4, 64], P('obs', 'state'), may hold values from 0 to 7
- block_count: int32 [8, 4], P('obs', 'state'), may hold values from 32 to 64, as said below
Outputs:
- analysis: bfloat16 [4, 1024, 256], P('state', 'obs')
Inputs may be any that keep to these rules, and one draw needn't show every extreme that they name: `block_count`: some device has exactly 64 live slots in every draw.
All inputs are finite; a program needn't handle non-finite values.
Results may differ from a plain program's by a relative error of at most 0.009.
Values sent between devices are 32-bit elements; how exact they have to be, the bound alone decides.
A program may use at most 64 MiB of HBM per device.

v0:
```python
import math
import jax
import jax.numpy as jnp
from jax import lax
from jax.sharding import PartitionSpec as P

K = 256
BS = 128
M_DEV = 2048
BLK_DEV = 64


def on_device(ensemble, obs_values, obs_error, h_blocks, block_rows, block_cols, block_count):
    members = ensemble[0]
    slab_rows = members.shape[0]
    state_blocks = slab_rows // BS
    obs_blocks = M_DEV // BS
    member_blocks = members.reshape(state_blocks, BS, K)
    group_size = math.gcd(BLK_DEV, 32)
    group_count = BLK_DEV // group_size
    all_blocks = h_blocks[0, 0]
    all_cols = block_cols[0, 0]
    all_rows = block_rows[0, 0]
    live_count = block_count[0, 0]
    block_ids = jnp.arange(obs_blocks, dtype=jnp.int32)

    def add_group(group_index, carry):
        start = (group_index * group_size).astype(jnp.int32)
        blocks = lax.dynamic_slice_in_dim(all_blocks, start, group_size, 0)
        cols = lax.dynamic_slice_in_dim(all_cols, start, group_size, 0)
        rows = lax.dynamic_slice_in_dim(all_rows, start, group_size, 0)
        live_mask = start + jnp.arange(group_size, dtype=jnp.int32) < live_count
        picked = member_blocks[cols]
        products = jnp.einsum("bij,bjk->bik", blocks, picked, preferred_element_type=jnp.float32)
        upper_part = products.astype(jnp.bfloat16)
        lower_part = (products - upper_part.astype(jnp.float32)).astype(jnp.bfloat16)
        onehot = ((rows[None, :] == block_ids[:, None]) & live_mask[None, :]).astype(jnp.bfloat16)
        carry = carry + jnp.einsum(
            "mb,bik->mik", onehot, upper_part, preferred_element_type=jnp.float32
        )
        carry = carry + jnp.einsum(
            "mb,bik->mik", onehot, lower_part, preferred_element_type=jnp.float32
        )
        return carry

    accumulated = lax.fori_loop(
        0, group_count, add_group, jnp.zeros((obs_blocks, BS, K), jnp.float32)
    )
    slab_term = accumulated.reshape(M_DEV, K)
    state_devices = lax.axis_size("state")
    rows_share = M_DEV // state_devices
    row_offset = lax.axis_index("state") * rows_share
    own_rows = lax.psum_scatter(slab_term, "state", scatter_dimension=0, tiled=True)
    own_values = lax.dynamic_slice_in_dim(obs_values, row_offset, rows_share, 0)
    own_errors = lax.dynamic_slice_in_dim(obs_error, row_offset, rows_share, 0)
    obs_mean = jnp.mean(own_rows, axis=1)
    whitened = (own_rows - obs_mean[:, None]) / own_errors[:, None]
    innovation = (own_values - obs_mean) / own_errors
    gram_part = lax.dot_general(
        whitened, whitened, (((0,), (0,)), ((), ())), precision=lax.Precision.HIGHEST
    )
    projected_part = jnp.dot(innovation, whitened, precision=lax.Precision.HIGHEST)
    identity = jnp.eye(K, dtype=jnp.float32)
    gram_sum, projected_innovation = lax.psum((gram_part, projected_part), ("obs", "state"))
    lower_factor = jnp.linalg.cholesky(gram_sum + (K - 1) * identity)
    halfway = lax.linalg.triangular_solve(
        lower_factor, projected_innovation[:, None], left_side=True, lower=True
    )
    mean_weight = lax.linalg.triangular_solve(
        lower_factor, halfway, left_side=True, lower=True, transpose_a=True
    )
    root_inverse = lax.linalg.triangular_solve(
        lower_factor, identity, left_side=True, lower=True, transpose_a=True
    )
    transform = (math.sqrt(K - 1) * root_inverse + mean_weight).astype(jnp.bfloat16)
    piece_rows = slab_rows // lax.axis_size("obs")
    own_piece = lax.dynamic_slice_in_dim(
        members, lax.axis_index("obs") * piece_rows, piece_rows, 0
    ).astype(jnp.float32)
    state_mean = jnp.mean(own_piece, axis=1)
    anomalies = (own_piece - state_mean[:, None]).astype(jnp.bfloat16)
    analysis = state_mean[:, None] + jnp.dot(
        anomalies, transform, preferred_element_type=jnp.float32
    )
    return analysis.astype(jnp.bfloat16)[None]


def solution(mesh):
    placed = (
        P("state", None, None),
        P("obs"),
        P("obs"),
        P("obs", "state", None, None, None),
        P("obs", "state", None),
        P("obs", "state", None),
        P("obs", "state"),
    )
    return jax.shard_map(
        on_device, mesh=mesh, in_specs=placed, out_specs=P("state", "obs", None), check_vma=False
    )
```

profile of v0, /device:TPU:0, one launch (start us, length us, event | category | flops | bytes accessed | tf_op | source)
XLA Modules:
  0.0 278.9 jit_solution(10647405630408804250)
XLA Ops:
  6.5 24.7 %while.16 = (s32[]{:T(128)}, f32[16,128,256]{2,0,1:T(8,128)}, s32[64]{0:T(128)}, s32[]{:T(128)}, bf16[64,128,128]{2,1,0:T(8,128)(2,1)}, /*index=5*/s32[64]{0:T(1...) while((s32[]{:T(128)}, f32[16,128,256]{2,0,1:T(8,128)}, ...), condition=%wide.region_2.0_spmd.clone, body=%wide.region_1.0_spmd.clone.sunk | while | flops 341314720 | bytes 24123700 | solution.py:46
  7.3 1.7 gather_fusion
  9.0 3.2 %subtract_convert_fusion.2 = (bf16[32,128,256]{2,1,0:T(8,128)(2,1)S(1)}, bf16[32,128,256]{2,1,0:T(8,128)(2,1)}) fusion(bf16[32,128,256]{2,1,0:T(8,128)(2,1)S(1)} %gather_fusion, bf16[64,128,128]{2,1,0:T(8,128)(2,1)} %get-tuple-element.322, s32[]{:T(128)S(6)} %select_n.37), kind=kOutput, calls=%fused_computation.4.clone.1 | convolution fusion | flops 272629760 | bytes 7340036 | tf_op jit(solution)/shard_map/while/body/eval_jaxpr/bij,bjk->bik/dot_general | solution.py:34
  13.0 1.3 fusion.80
  14.2 4.3 %fusion.81 = f32[16,128,256]{2,0,1:T(8,128)} fusion(f32[16,128,256]{2,0,1:T(8,128)S(1)} %fusion.80, f32[16,128,256]{2,0,1:T(8,128)} %get-tuple-element.308, bf16[32,128,256]{2,1,0:T(8,128)(2,1)} %get-tuple-element.295, pred[]{:T(512)S(6)} %compare.30, s32[32]{0:T(128)S(1)} %dynamic_slice.54, pred[32]{0:T(512)(128)(4,1)S(1)} %add_compare_fusion.2), kind=kOutput, calls=%fused_computation.10.clone.1 | convolution fusion | flops 35128320 | bytes 8388769 | tf_op jit(solution)/shard_map/while/body/eval_jaxpr/mb,bik->mik/dot_general | solution.py:38
  19.3 1.7 gather_fusion
  21.0 3.2 %subtract_convert_fusion.2 = (bf16[32,128,256]{2,1,0:T(8,128)(2,1)S(1)}, bf16[32,128,256]{2,1,0:T(8,128)(2,1)}) fusion(bf16[32,128,256]{2,1,0:T(8,128)(2,1)S(1)} %gather_fusion, bf16[64,128,128]{2,1,0:T(8,128)(2,1)} %get-tuple-element.322, s32[]{:T(128)S(6)} %select_n.37), kind=kOutput, calls=%fused_computation.4.clone.1 | convolution fusion | flops 272629760 | bytes 7340036 | tf_op jit(solution)/shard_map/while/body/eval_jaxpr/bij,bjk->bik/dot_general | solution.py:34
  25.0 1.3 fusion.80
  26.3 5.0 %fusion.81 = f32[16,128,256]{2,0,1:T(8,128)} fusion(f32[16,128,256]{2,0,1:T(8,128)S(1)} %fusion.80, f32[16,128,256]{2,0,1:T(8,128)} %get-tuple-element.308, bf16[32,128,256]{2,1,0:T(8,128)(2,1)} %get-tuple-element.295, pred[]{:T(512)S(6)} %compare.30, s32[32]{0:T(128)S(1)} %dynamic_slice.54, pred[32]{0:T(512)(128)(4,1)S(1)} %add_compare_fusion.2), kind=kOutput, calls=%fused_computation.10.clone.1 | convolution fusion | flops 35128320 | bytes 8388769 | tf_op jit(solution)/shard_map/while/body/eval_jaxpr/mb,bik->mik/dot_general | solution.py:38
  31.2 4.1 %copy.18 = f32[16,128,256]{2,1,0:T(8,128)} copy(f32[16,128,256]{2,0,1:T(8,128)} %get-tuple-element.144) | data formatting | bytes 4194304 | tf_op jit(solution)/shard_map/while | solution.py:46
  36.4 37.0 %reduce-scatter.2.cloned.1.call-done = f32[512,256]{1,0:T(8,128)} async-done(((f32[2048,256]{1,0:T(8,128)}), f32[512,256]{1,0:T(8,128)}) %reduce-scatter.2.cloned.1.call-update) | async-done | bytes 524304 | tf_op jit(solution)/shard_map/reduce_scatter | solution.py:53
  73.4 1.3 reduce_sum.19
  75.5 3.2 %fusion.54 = f32[256,256]{0,1:T(8,128)} fusion(f32[512,256]{1,0:T(8,128)} %reduce-scatter.2.cloned.1.call-done, f32[512]{0:T(512)S(1)} %get-tuple-element.216, f32[512]{0:T(512)S(1)} %get-tuple-element.217), kind=kOutput, calls=%fused_computation.89 | convolution fusion | flops 402915328 | bytes 790528 | tf_op jit(solution)/shard_map/dot_general | solution.py:59
  79.2 39.5 %psum.15 = f32[256]{0:T(256)S(1)} all-reduce(f32[256]{0:T(256)S(1)} %bitcast.108), channel_id=1, replica_groups=mesh['obs'=8,'state'=4] {'obs','state'}, use_global_device_ids=true, to_apply=%region_10.11 | all-reduce | flops 256 | bytes 2048 | tf_op jit(solution)/shard_map/psum | solution.py:64
  118.6 87.0 %all-reduce.3.cloned.1.call-done = f32[256,256]{0,1:T(8,128)} async-done(((f32[256,256]{0,1:T(8,128)}), f32[256,256]{0,1:T(8,128)}) %all-reduce.3.cloned.1.call-update) | async-done | bytes 262160 | tf_op jit(solution)/shard_map/psum | solution.py:64
  206.7 1.0 fusion.28
  207.7 11.7 %cholesky.49 = f32[128,128]{1,0:T(8,128)S(1)} custom-call(f32[128,128]{1,0:T(8,128)S(1)} %cholesky.115), custom_call_target="Cholesky" | custom-call | tf_op jit(solution)/shard_map/jit(cholesky)/cholesky | solution.py:65
  219.5 9.8 %custom-call.18 = f32[1,128,128]{1,2,0:T(8,128)S(1)} custom-call(f32[1,128,128]{2,1,0:T(8,128)S(1)} %get-tuple-element.214), custom_call_target="InvertDiagBlocksLowerTriangular" | custom-call | tf_op jit(solution)/shard_map/jit(cholesky)/cholesky | solution.py:65
  229.8 11.7 %cholesky.103 = f32[128,128]{1,0:T(8,128)S(1)} custom-call(f32[128,128]{1,0:T(8,128)S(1)} %convolution_subtract_fusion.1), custom_call_target="Cholesky" | custom-call | tf_op jit(solution)/shard_map/jit(cholesky)/cholesky | solution.py:65
  244.0 4.3 %while.15 = (s32[]{:T(128)}, f32[256,256]{0,1:T(8,128)S(1)}, s32[2,2]{1,0:T(2,128)S(1)}, f32[2,128,128]{2,1,0:T(8,128)S(1)}, s32[]{:T(128)}) while((s32[]{:T(128)}, f32[256,256]{0,1:T(8,128)S(1)}, s32[2,2]{1,0:T(2,128)S(1)}, f32[2,128,128]{2,1,0:T(8,128)S(1)}, s32[]{:T(128)}) %tuple.58), condition=%wide.while_cond, body=%wide.while_body.sunk | while | flops 2 | bytes 393321 | solution.py:72
  244.6 1.3 dynamic-slice.8
  246.8 1.3 dynamic-slice.8
  248.3 19.9 %custom-call.19 = f32[2,128,128]{1,2,0:T(8,128)S(1)} custom-call(f32[2,128,128]{2,1,0:T(8,128)S(1)} %get-tuple-element.152), custom_call_target="InvertDiagBlocksLowerTriangular" | custom-call | tf_op jit(solution)/shard_map/triangular_solve | solution.py:72
  270.3 1.7 fusion.21
  (60 shorter events, 11.6 us)
Async XLA Ops:
  6.5 66.9 %reduce-scatter.2.cloned.1.call-start = ((), (), s32[]{:S(2)}) async-start(), calls=%async_computation.1 | async-start | bytes 2621440 | tf_op jit(solution)/shard_map/reduce_scatter | solution.py:53
  9.0 3.2 %copy-start.1 = (s32[64]{0:T(128)S(1)}, s32[64]{0:T(128)}, u32[]{:S(2)}) copy-start(s32[64]{0:T(128)} %get-tuple-element.320) | copy-start | bytes 772 | tf_op jit(solution)/shard_map/while
  21.0 3.2 %copy-start.1 = (s32[64]{0:T(128)S(1)}, s32[64]{0:T(128)}, u32[]{:S(2)}) copy-start(s32[64]{0:T(128)} %get-tuple-element.320) | copy-start | bytes 772 | tf_op jit(solution)/shard_map/while
  35.4 170.3 %all-reduce.3.cloned.1.call-start = ((), (), s32[]{:S(2)}) async-start(), calls=%async_computation.2 | async-start | bytes 524288 | tf_op jit(solution)/shard_map/psum | solution.py:64
  73.4 5.3 %copy-start = (f32[512,256]{1,0:T(8,128)S(1)}, f32[512,256]{1,0:T(8,128)}, u32[]{:S(2)}) copy-start(f32[512,256]{1,0:T(8,128)} %reduce-scatter.2.cloned.1.call-done) | copy-start | bytes 1572868
Sparse Core Ops, SparseCore 0:
  35.5 37.9 reduce-scatter.1
  78.9 126.6 all-reduce.2
where the time goes:
time: 280 us; the launch traced here: 279 us
  waiting for transfers between devices  124 us (44%)
  other arithmetic  61.7 us (22%)
  blocking collectives  39.5 us (14%)
  matrix products  26.2 us (9%)
  between operations  14.9 us (5%)
  local copies, waits for them, and re-layouts  12.4 us (4%)
    psum x1, waiting for transfers between devices, on_device(): lax.psum((gram_part, projected_part), ('obs', 'state'))  87 us
    psum x1, blocking collectives, on_device(): lax.psum((gram_part, projected_part), ('obs', 'state'))  39.5 us
    reduce_scatter x1, waiting for transfers between devices, on_device(): lax.psum_scatter(slab_term, 'state', scatter_dimension=0, tiled=True)  37 us
    another operation x6, other arithmetic, on_device(): lower_factor = jnp.linalg.cholesky(gram_sum + (K - 1) * identity)  34 us
    another operation x3, other arithmetic, on_device(): lax.linalg.triangular_solve(lower_factor, identity, left_side=True, lower...  19.9 us
    dot_general x2, matrix products, add_group(): jnp.einsum('mb,bik->mik', onehot, upper_part, preferred_element_type=jnp....  9.29 us
    dot_general x2, matrix products, add_group(): jnp.einsum('bij,bjk->bik', blocks, picked, preferred_element_type=jnp.flo...  6.45 us
  transfers between devices with their start and end apart: 2, of which 2 were waited for; matrix products, arithmetic and copies ran while one was open for 1% of the time, Pallas kernels for 0%

commit v1 on v0

--- a/solution.py
+++ b/solution.py
@@ -61,7 +61,7 @@
     )
     projected_part = jnp.dot(innovation, whitened, precision=lax.Precision.HIGHEST)
     identity = jnp.eye(K, dtype=jnp.float32)
-    gram_sum, projected_innovation = lax.psum((gram_part, projected_part), ("obs", "state"))
+    gram_sum, projected_innovation = lax.psum(lax.psum((gram_part, projected_part), "obs"), "state")
     lower_factor = jnp.linalg.cholesky(gram_sum + (K - 1) * identity)
     halfway = lax.linalg.triangular_solve(
         lower_factor, projected_innovation[:, None], left_side=True, lower=True

time: 280 us -> 253 us (0.904)
  blocking collectives: 39.5 us -> 23.7 us
  waiting for transfers between devices: 124 us -> 113 us
    psum x1 -> x2, blocking collectives: 39.5 us -> 23.7 us  [the longest x1 13.7 us: on_device(): lax.psum((gram_part, projected_part), 'obs')]
    psum x1 -> x2, waiting for transfers between devices: 87 us -> 76.3 us  [the longest x1 55.5 us: on_device(): lax.psum((gram_part, projected_part), 'obs')]
  transfers between devices with their start and end apart: 2 -> 3, of which waited for: 2 -> 3; matrix products, arithmetic and copies ran while one was open for 1% -> 1% of each run, Pallas kernels for 0% -> 0%
where the time goes in v1:
time: 253 us; the launch traced here: 252 us
  waiting for transfers between devices  113 us (45%)
  other arithmetic  61.7 us (24%)
  matrix products  26.2 us (10%)
  blocking collectives  23.7 us (9%)
  between operations  14.6 us (6%)
  local copies, waits for them, and re-layouts  12.4 us (5%)
    psum x1, waiting for transfers between devices, on_device(): lax.psum((gram_part, projected_part), 'obs')  55.5 us
    reduce_scatter x1, waiting for transfers between devices, on_device(): lax.psum_scatter(slab_term, 'state', scatter_dimension=0, tiled=True)  37.1 us
    another operation x6, other arithmetic, on_device(): lower_factor = jnp.linalg.cholesky(gram_sum + (K - 1) * identity)  34 us
    psum x1, waiting for transfers between devices, on_device(): lax.psum(lax.psum((gram_part, projected_part), 'obs'), 'state')  20.9 us
    another operation x3, other arithmetic, on_device(): lax.linalg.triangular_solve(lower_factor, identity, left_side=True, lower...  19.9 us
    psum x1, blocking collectives, on_device(): lax.psum((gram_part, projected_part), 'obs')  13.7 us
    psum x1, blocking collectives, on_device(): lax.psum(lax.psum((gram_part, projected_part), 'obs'), 'state')  10 us
    dot_general x2, matrix products, add_group(): jnp.einsum('mb,bik->mik', onehot, upper_part, preferred_element_type=jnp....  9.29 us
  transfers between devices with their start and end apart: 3, of which 3 were waited for; matrix products, arithmetic and copies ran while one was open for 1% of the time, Pallas kernels for 0%

profile of v1, /device:TPU:0, one launch (start us, length us, event | category | flops | bytes accessed | tf_op | source)
XLA Modules:
  0.0 252.3 jit_solution(18180711492368565137)
XLA Ops:
  6.5 24.7 %while.16 = (s32[]{:T(128)}, f32[16,128,256]{2,0,1:T(8,128)}, s32[64]{0:T(128)}, s32[]{:T(128)}, bf16[64,128,128]{2,1,0:T(8,128)(2,1)}, /*index=5*/s32[64]{0:T(1...) while((s32[]{:T(128)}, f32[16,128,256]{2,0,1:T(8,128)}, ...), condition=%wide.region_2.0_spmd.clone, body=%wide.region_1.0_spmd.clone.sunk | while | flops 341314720 | bytes 24123700 | solution.py:46
  7.3 1.7 gather_fusion
  9.0 3.2 %subtract_convert_fusion.2 = (bf16[32,128,256]{2,1,0:T(8,128)(2,1)S(1)}, bf16[32,128,256]{2,1,0:T(8,128)(2,1)}) fusion(bf16[32,128,256]{2,1,0:T(8,128)(2,1)S(1)} %gather_fusion, bf16[64,128,128]{2,1,0:T(8,128)(2,1)} %get-tuple-element.322, s32[]{:T(128)S(6)} %select_n.37), kind=kOutput, calls=%fused_computation.4.clone.1 | convolution fusion | flops 272629760 | bytes 7340036 | tf_op jit(solution)/shard_map/while/body/eval_jaxpr/bij,bjk->bik/dot_general | solution.py:34
  13.0 1.3 fusion.80
  14.2 4.3 %fusion.81 = f32[16,128,256]{2,0,1:T(8,128)} fusion(f32[16,128,256]{2,0,1:T(8,128)S(1)} %fusion.80, f32[16,128,256]{2,0,1:T(8,128)} %get-tuple-element.308, bf16[32,128,256]{2,1,0:T(8,128)(2,1)} %get-tuple-element.295, pred[]{:T(512)S(6)} %compare.30, s32[32]{0:T(128)S(1)} %dynamic_slice.54, pred[32]{0:T(512)(128)(4,1)S(1)} %add_compare_fusion.2), kind=kOutput, calls=%fused_computation.10.clone.1 | convolution fusion | flops 35128320 | bytes 8388769 | tf_op jit(solution)/shard_map/while/body/eval_jaxpr/mb,bik->mik/dot_general | solution.py:38
  19.3 1.7 gather_fusion
  21.0 3.2 %subtract_convert_fusion.2 = (bf16[32,128,256]{2,1,0:T(8,128)(2,1)S(1)}, bf16[32,128,256]{2,1,0:T(8,128)(2,1)}) fusion(bf16[32,128,256]{2,1,0:T(8,128)(2,1)S(1)} %gather_fusion, bf16[64,128,128]{2,1,0:T(8,128)(2,1)} %get-tuple-element.322, s32[]{:T(128)S(6)} %select_n.37), kind=kOutput, calls=%fused_computation.4.clone.1 | convolution fusion | flops 272629760 | bytes 7340036 | tf_op jit(solution)/shard_map/while/body/eval_jaxpr/bij,bjk->bik/dot_general | solution.py:34
  25.0 1.3 fusion.80
  26.3 5.0 %fusion.81 = f32[16,128,256]{2,0,1:T(8,128)} fusion(f32[16,128,256]{2,0,1:T(8,128)S(1)} %fusion.80, f32[16,128,256]{2,0,1:T(8,128)} %get-tuple-element.308, bf16[32,128,256]{2,1,0:T(8,128)(2,1)} %get-tuple-element.295, pred[]{:T(512)S(6)} %compare.30, s32[32]{0:T(128)S(1)} %dynamic_slice.54, pred[32]{0:T(512)(128)(4,1)S(1)} %add_compare_fusion.2), kind=kOutput, calls=%fused_computation.10.clone.1 | convolution fusion | flops 35128320 | bytes 8388769 | tf_op jit(solution)/shard_map/while/body/eval_jaxpr/mb,bik->mik/dot_general | solution.py:38
  31.2 4.1 %copy.18 = f32[16,128,256]{2,1,0:T(8,128)} copy(f32[16,128,256]{2,0,1:T(8,128)} %get-tuple-element.144) | data formatting | bytes 4194304 | tf_op jit(solution)/shard_map/while | solution.py:46
  36.4 37.1 %reduce-scatter.2.cloned.1.call-done = f32[512,256]{1,0:T(8,128)} async-done(((f32[2048,256]{1,0:T(8,128)}), f32[512,256]{1,0:T(8,128)}) %reduce-scatter.2.cloned.1.call-update) | async-done | bytes 524304 | tf_op jit(solution)/shard_map/reduce_scatter | solution.py:53
  75.5 3.2 %fusion.54 = f32[256,256]{0,1:T(8,128)} fusion(f32[512,256]{1,0:T(8,128)} %reduce-scatter.2.cloned.1.call-done, f32[512]{0:T(512)S(1)} %get-tuple-element.216, f32[512]{0:T(512)S(1)} %get-tuple-element.217), kind=kOutput, calls=%fused_computation.89 | convolution fusion | flops 402915328 | bytes 790528 | tf_op jit(solution)/shard_map/dot_general | solution.py:59
  78.8 55.5 %all-reduce.4.cloned.1.call-done = f32[256,256]{0,1:T(8,128)} async-done(((f32[256,256]{0,1:T(8,128)}), f32[256,256]{0,1:T(8,128)}) %all-reduce.4.cloned.1.call-update) | async-done | bytes 262160 | tf_op jit(solution)/shard_map/psum | solution.py:64
  134.8 13.7 %psum.30 = f32[256]{0:T(256)S(1)} all-reduce(f32[256]{0:T(256)S(1)} %bitcast.108), channel_id=1, replica_groups=mesh['obs'=8,'state'=4] {'obs'}, use_global_device_ids=true, to_apply=%region_11.12 | all-reduce | flops 256 | bytes 2048 | tf_op jit(solution)/shard_map/psum | solution.py:64
  148.5 10.0 %psum.31 = f32[256]{0:T(256)S(1)} all-reduce(f32[256]{0:T(256)S(1)} %psum.30), channel_id=1, replica_groups=mesh['obs'=8,'state'=4] {'state'}, use_global_device_ids=true, to_apply=%region_12.13 | all-reduce | flops 256 | bytes 2048 | tf_op jit(solution)/shard_map/psum | solution.py:64
  158.5 20.9 %all-reduce.6.cloned.1.call-done = f32[256,256]{0,1:T(8,128)} async-done(((f32[256,256]{0,1:T(8,128)}), f32[256,256]{0,1:T(8,128)}) %all-reduce.6.cloned.1.call-update) | async-done | bytes 262160 | tf_op jit(solution)/shard_map/psum | solution.py:64
  181.5 11.7 %cholesky.49 = f32[128,128]{1,0:T(8,128)S(1)} custom-call(f32[128,128]{1,0:T(8,128)S(1)} %cholesky.115), custom_call_target="Cholesky" | custom-call | tf_op jit(solution)/shard_map/jit(cholesky)/cholesky | solution.py:65
  193.2 9.8 %custom-call.18 = f32[1,128,128]{1,2,0:T(8,128)S(1)} custom-call(f32[1,128,128]{2,1,0:T(8,128)S(1)} %get-tuple-element.214), custom_call_target="InvertDiagBlocksLowerTriangular" | custom-call | tf_op jit(solution)/shard_map/jit(cholesky)/cholesky | solution.py:65
  203.5 11.7 %cholesky.103 = f32[128,128]{1,0:T(8,128)S(1)} custom-call(f32[128,128]{1,0:T(8,128)S(1)} %convolution_subtract_fusion.1), custom_call_target="Cholesky" | custom-call | tf_op jit(solution)/shard_map/jit(cholesky)/cholesky | solution.py:65
  217.7 4.3 %while.15 = (s32[]{:T(128)}, f32[256,256]{0,1:T(8,128)S(1)}, s32[2,2]{1,0:T(2,128)S(1)}, f32[2,128,128]{2,1,0:T(8,128)S(1)}, s32[]{:T(128)}) while((s32[]{:T(128)}, f32[256,256]{0,1:T(8,128)S(1)}, s32[2,2]{1,0:T(2,128)S(1)}, f32[2,128,128]{2,1,0:T(8,128)S(1)}, s32[]{:T(128)}) %tuple.58), condition=%wide.while_cond, body=%wide.while_body.sunk | while | flops 2 | bytes 393321 | solution.py:72
  218.4 1.3 dynamic-slice.8
  220.5 1.3 dynamic-slice.8
  222.0 19.9 %custom-call.19 = f32[2,128,128]{1,2,0:T(8,128)S(1)} custom-call(f32[2,128,128]{2,1,0:T(8,128)S(1)} %get-tuple-element.152), custom_call_target="InvertDiagBlocksLowerTriangular" | custom-call | tf_op jit(solution)/shard_map/triangular_solve | solution.py:72
  244.0 1.7 fusion.21
  (64 shorter events, 13.9 us)
Async XLA Ops:
  6.5 66.9 %reduce-scatter.2.cloned.1.call-start = ((), (), s32[]{:S(2)}) async-start(), calls=%async_computation.1 | async-start | bytes 2621440 | tf_op jit(solution)/shard_map/reduce_scatter | solution.py:53
  9.0 3.2 %copy-start.1 = (s32[64]{0:T(128)S(1)}, s32[64]{0:T(128)}, u32[]{:S(2)}) copy-start(s32[64]{0:T(128)} %get-tuple-element.320) | copy-start | bytes 772 | tf_op jit(solution)/shard_map/while
  21.0 3.2 %copy-start.1 = (s32[64]{0:T(128)S(1)}, s32[64]{0:T(128)}, u32[]{:S(2)}) copy-start(s32[64]{0:T(128)} %get-tuple-element.320) | copy-start | bytes 772 | tf_op jit(solution)/shard_map/while
  35.4 98.9 %all-reduce.4.cloned.1.call-start = ((), (), s32[]{:S(2)}) async-start(), calls=%async_computation.2 | async-start | bytes 524288 | tf_op jit(solution)/shard_map/psum | solution.py:64
  73.4 60.9 %copy-start = (f32[512,256]{1,0:T(8,128)S(1)}, f32[512,256]{1,0:T(8,128)}, u32[]{:S(2)}) copy-start(f32[512,256]{1,0:T(8,128)} %reduce-scatter.2.cloned.1.call-done) | copy-start | bytes 1572868
  78.7 100.6 %all-reduce.6.cloned.1.call-start = ((), (), s32[]{:S(2)}) async-start(), calls=%async_computation.3 | async-start | bytes 524288 | tf_op jit(solution)/shard_map/psum | solution.py:64
Sparse Core Ops, SparseCore 0:
  35.5 37.9 reduce-scatter.1
  78.9 55.3 all-reduce.3
  137.2 42.0 all-reduce.5
